TPU v7x, 256 devices: a whole 4x4x8 slice. The times are simulated.
256 devices in a mesh: lon: 16 (over y, x), lat: 8 (over z), mem: 2 (over core).
Axes of the slice: x: 4, y: 4, z: 8, core: 2. Of those that a mesh axis runs over, the one named last changes fastest.
Arguments:
- anomalies: bfloat16 [128, 128, 4096], P('mem', 'lat', 'lon'), may hold values from -6 to 6
- state_mean: float32 [128, 4096], P('lat', 'lon'), may hold values from -6 to 6
- delayed_deviation_pair: bfloat16 [2, 128, 128, 4096], P(None, 'mem', 'lat', 'lon'), may hold values from -6 to 6
- lagged_means: float32 [2, 128, 4096], P(None, 'lat', 'lon'), may hold values from -6 to 6
- courant_lon: float32 [128, 4096], P('lat', 'lon'), may hold values from -0.45 to 0.45
- courant_lat: float32 [128, 4096], P('lat', 'lon'), may hold values from -0.45 to 0.45
- ocean: int32 [128, 4096], P('lat', 'lon'), may hold values 0 or 1
- obs_values: float32 [16384, 64], P(('lon', 'lat')), may hold values from -160 to 160
- obs_variance: float32 [16384, 64], P(('lon', 'lat')), may hold values from 2048 to 32768
- obs_cells: int32 [16384, 64], P(('lon', 'lat')), may hold values from 0 to 4095
- obs_tile: int32 [16384, 1], P(('lon', 'lat')), may hold values from 0 to 127; in each aligned block of 128 rows (0 to 127, 128 to 255, ...) at most 2 rows name the same one
- obs_count: int32 [16384], P(('lon', 'lat')), may hold values from 48 to 64
Outputs:
- analysis_anomalies: bfloat16 [3, 128, 128, 4096], P(None, 'mem', 'lat', 'lon')
- analysis_mean: float32 [3, 128, 4096], P(None, 'lat', 'lon')
Inputs may be any that keep to these rules, and one draw needn't show every extreme that they name: `obs_tile`: among the 128 blocks of one tile (an aligned run of rows) no tile is named more than 2 times.
All inputs are finite; a program needn't handle non-finite values. Where the computation divides by a largest or mean magnitude, that divisor is 1e-20 or more. No bound on the sum of `ocean` on one device may be relied on, other than what follows from the above.
Results may differ from a plain program's by a relative error of at most 0.0034.
Values may be sent and summed in bfloat16 or wider, within the bound.
A program may use at most 64 MiB of HBM per device.

v0:
```python
import math
import jax
import jax.numpy as jnp
from jax import lax
from jax.sharding import Mesh
from jax.sharding import PartitionSpec as P

SUBSTEPS = 4
NS_ITERS = 8
LON = ("lon_0", "lon_1")
LON_LAT = ("lon_0", "lon_1", "lat")


def with_halo(x, sides, width, wrap):
    for axis, dim in sides:
        count, length = (lax.axis_size(axis), x.shape[dim])
        up = [(i, (i + 1) % count) for i in range(count if wrap else count - 1)]
        down = [(j, i) for i, j in up]
        last = lax.slice_in_dim(x, length - width, length, axis=dim)
        leading = lax.slice_in_dim(x, 0, width, axis=dim)
        before = lax.ppermute(last, axis, up)
        after = lax.ppermute(leading, axis, down)
        x = jnp.concatenate([before, x, after], axis=dim)
    return x


def sent_together(arrays, axis, split_dim, concat_dim, along):
    widths = [a.shape[along] for a in arrays]
    both = jnp.concatenate(arrays, axis=along)
    out = lax.all_to_all(both, axis, split_axis=split_dim, concat_axis=concat_dim, tiled=True)
    return tuple(jnp.split(out, [sum(widths[:k]) for k in range(1, len(widths))], axis=along))


def over_axes(x, axes):
    for axis in axes:
        x = lax.psum(x, axis)
    return x


def side_by_side(arrays, axis, dim, along):
    widths = [math.prod(a.shape[along:]) for a in arrays]
    both = jnp.concatenate(
        [a.reshape(*a.shape[:along], w) for a, w in zip(arrays, widths)], axis=along
    )
    out = lax.all_gather(both, axis, axis=dim, tiled=True)
    blocks = jnp.split(out, [sum(widths[:k]) for k in range(1, len(widths))], axis=along)
    return tuple((b.reshape(*out.shape[:along], *a.shape[along:]) for a, b in zip(arrays, blocks)))


def upwind(center, western, eastern, southern, northern, courant_x, courant_y, wet_mask):
    tendency = (
        jnp.maximum(courant_x, 0.0) * (center - western)
        + jnp.minimum(courant_x, 0.0) * (eastern - center)
        + jnp.maximum(courant_y, 0.0) * (center - southern)
        + jnp.minimum(courant_y, 0.0) * (northern - center)
    )
    return center - wet_mask * tendency


def inverse_root(gram, projection):
    members = gram.shape[0]
    identity = jnp.eye(members, dtype=jnp.float32)
    system = (members - 1.0) * identity + 0.5 * (gram + gram.T)
    bound = jnp.max(jnp.sum(jnp.abs(system), axis=1))
    iterate = system / bound
    accum = identity
    for sweep in range(NS_ITERS):
        factor = 1.5 * identity - 0.5 * jnp.dot(accum, iterate, precision=lax.Precision.HIGHEST)
        iterate = jnp.dot(iterate, factor, precision=lax.Precision.HIGHEST)
        accum = jnp.dot(factor, accum, precision=lax.Precision.HIGHEST)
    root = accum / jnp.sqrt(bound)
    weights = jnp.dot(
        root,
        jnp.dot(root, projection, precision=lax.Precision.HIGHEST),
        precision=lax.Precision.HIGHEST,
    )
    transform = jnp.sqrt(members - 1.0) * root
    return (transform.astype(jnp.bfloat16), weights.astype(jnp.bfloat16))


def body(
    anomalies,
    state_mean,
    delayed_deviation_pair,
    lagged_means,
    courant_lon,
    courant_lat,
    ocean,
    obs_values,
    obs_variance,
    obs_cells,
    obs_tile,
    obs_count,
):
    locally_held_samples = anomalies.shape[0]
    wet_mask = ocean.astype(jnp.float32)
    coefficients = jnp.stack([courant_lon, courant_lat, wet_mask])
    sample_surfaces = jnp.concatenate([anomalies.astype(jnp.float32), state_mean[None]], 0)
    stacked = jnp.concatenate([sample_surfaces, coefficients], 0)
    widened = with_halo(stacked, ((LON, 2),), SUBSTEPS, True)
    extended = with_halo(widened.astype(jnp.bfloat16), (("lat", 1),), SUBSTEPS, False).astype(
        widened.dtype
    )
    field_count = sample_surfaces.shape[0]
    sample_surfaces = extended[:field_count]
    beside_all = extended[field_count:]
    for substep in range(SUBSTEPS):
        inner = beside_all[
            :,
            substep + 1 : beside_all.shape[1] - substep - 1,
            substep + 1 : beside_all.shape[2] - substep - 1,
        ]
        sample_surfaces = upwind(
            sample_surfaces[:, 1:-1, 1:-1],
            sample_surfaces[:, 1:-1, :-2],
            sample_surfaces[:, 1:-1, 2:],
            sample_surfaces[:, :-2, 1:-1],
            sample_surfaces[:, 2:, 1:-1],
            inner[0],
            inner[1],
            inner[2],
        )
    predicted_sample_vectors = sample_surfaces[:locally_held_samples].astype(jnp.bfloat16)
    prior_mean = sample_surfaces[locally_held_samples]
    total_cells = prior_mean.shape[0] * prior_mean.shape[1]
    tiles = lax.axis_size(LON_LAT)
    block_total = obs_values.shape[0]
    slot_width = obs_values.shape[1]
    capacity = 2 * block_total // tiles
    target = obs_tile[:, 0]
    block_order = jnp.arange(block_total, dtype=jnp.int32)
    same_target = target[:, None] == target[None, :]
    earlier = block_order[:, None] > block_order[None, :]
    position = jnp.sum((same_target & earlier).astype(jnp.int32), 1)
    destination = target * capacity + position
    placement_table = (
        destination[:, None] == jnp.arange(tiles * capacity, dtype=jnp.int32)[None, :]
    ).astype(jnp.float32)
    valid = jnp.arange(slot_width, dtype=jnp.int32)[None, :] < obs_count[:, None]
    weight = jnp.where(valid, 1.0 / obs_variance, 0.0)
    packed = jnp.concatenate([obs_values, weight, obs_cells.astype(jnp.float32)], 1)
    placed = lax.dot_general(
        placement_table, packed, (((0,), (0,)), ((), ())), precision=lax.Precision.HIGHEST
    ).reshape(tiles, capacity, 3, slot_width)
    arrived_values = sent_together(
        (placed[:, :, 0], placed[:, :, 1], placed[:, :, 2]), LON_LAT, 0, 0, 1
    )
    grid_cells = arrived_values[2].reshape(-1).astype(jnp.int32)
    obs_weight = arrived_values[1].reshape(-1)
    scaled_value = obs_weight * arrived_values[0].reshape(-1)
    rows, columns = (prior_mean.shape[0], prior_mean.shape[1])
    planes = []
    for plane in (obs_weight, scaled_value):
        upper = plane.astype(jnp.bfloat16)
        planes += [upper, (plane - upper.astype(jnp.float32)).astype(jnp.bfloat16)]
    in_row = (grid_cells // columns)[None, :] == jnp.arange(rows, dtype=jnp.int32)[:, None]
    in_column = (grid_cells % columns)[None, :] == jnp.arange(columns, dtype=jnp.int32)[:, None]
    spread = jnp.concatenate(
        [jnp.where(in_row, p[None, :], jnp.zeros((), jnp.bfloat16)) for p in planes], 0
    )
    sums = lax.dot_general(
        spread,
        in_column.astype(jnp.bfloat16),
        (((1,), (1,)), ((), ())),
        preferred_element_type=jnp.float32,
    ).reshape(2, 2, rows, columns)
    cell_weight = sums[0, 0] + sums[0, 1]
    cell_misfit = sums[1, 0] + sums[1, 1] - cell_weight * prior_mean
    observed = predicted_sample_vectors.reshape(locally_held_samples, total_cells)
    weighted = (observed.astype(jnp.float32) * cell_weight.reshape(-1)).astype(jnp.bfloat16)
    observed_all = lax.all_gather(observed, "mem", axis=0, tiled=True)
    gram_part = lax.dot_general(
        weighted, observed_all, (((1,), (1,)), ((), ())), preferred_element_type=jnp.float32
    )
    projection_part = lax.dot_general(
        observed,
        cell_misfit.reshape(-1).astype(jnp.bfloat16),
        (((1,), (0,)), ((), ())),
        preferred_element_type=jnp.float32,
    )
    gram_part, projection_part = (
        over_axes(gram_part, LON_LAT),
        over_axes(projection_part, LON_LAT),
    )
    gram, projection = side_by_side((gram_part, projection_part), "mem", 0, 1)
    transform, weights = inverse_root(gram, projection)
    marine_sample_vectors = jnp.concatenate(
        [predicted_sample_vectors[None], delayed_deviation_pair], 0
    )
    flat_states = marine_sample_vectors.reshape(3, locally_held_samples, total_cells)
    first_member = lax.axis_index("mem") * locally_held_samples
    own_columns = lax.dynamic_slice_in_dim(transform, first_member, locally_held_samples, 1)
    segment = lax.all_gather(marine_sample_vectors, "mem", axis=1, tiled=True)
    length = segment.shape[1]
    flat_segment = segment.reshape(3, length, total_cells)
    moved_sum = jnp.einsum(
        "nk,snc->skc", own_columns, flat_segment, preferred_element_type=jnp.float32
    )
    increment_sum = jnp.einsum(
        "n,snc->sc", weights, flat_segment, preferred_element_type=jnp.float32
    )
    wet_flat = wet_mask.reshape(-1)
    states_float = flat_states.astype(jnp.float32)
    blended = (states_float + wet_flat * (moved_sum - states_float)).astype(jnp.bfloat16)
    analysis_anomalies = blended.reshape(marine_sample_vectors.shape)
    state_means = jnp.concatenate([prior_mean[None], lagged_means], 0)
    analysis_mean = state_means + wet_mask * increment_sum.reshape(state_means.shape)
    return (analysis_anomalies, analysis_mean)


def solution(mesh):
    finer = Mesh(
        mesh.devices.reshape(4, 4, mesh.shape["lat"], mesh.shape["mem"]),
        ("lon_0", "lon_1", "lat", "mem"),
    )
    return jax.shard_map(
        body,
        mesh=finer,
        in_specs=(
            P("mem", "lat", LON),
            P("lat", LON),
            P(None, "mem", "lat", LON),
            P(None, "lat", LON),
            P("lat", LON),
            P("lat", LON),
            P("lat", LON),
            P(LON_LAT, None),
            P(LON_LAT, None),
            P(LON_LAT, None),
            P(LON_LAT, None),
            P(LON_LAT),
        ),
        out_specs=(P(None, "mem", "lat", LON), P(None, "lat", LON)),
        check_vma=False,
    )
```

profile of v0, /device:TPU:1, one launch (start us, length us, event | category | flops | bytes accessed | tf_op | source)
XLA Modules:
  0.0 169.0 jit_solution(13560718712493647950)
XLA Ops:
  7.2 1.1 convert_dynamic-update-slice_fusion
  8.3 0.7 bitcast_dynamic-update-slice_fusion.3
  9.1 0.7 bitcast_dynamic-update-slice_fusion.2
  9.8 0.7 bitcast_dynamic-update-slice_fusion.1
  10.5 0.7 bitcast_dynamic-update-slice_fusion
  11.4 0.3 copy.67
  11.7 2.1 %collective-permute-start = (bf16[68,16,4]{0,1,2:T(8,128)(2,1)S(1)}, bf16[68,16,4]{0,1,2:T(8,128)(2,1)S(1)}, u32[]{:S(2)}, u32[]{:S(2)}) collective-permute-start(bf16[68,16,4]{0,1,2:T(8,128)(2,1)S(1)} %copy.67), channel_id=1, source_target_pairs={{0,16},{16,32},{32,48},{48,64},{64,80},{80,96},{96,112},{112,128},... | collective-permute-start | bytes 26120 | tf_op jit(solution)/shard_map/ppermute | solution.py:21
  13.8 0.3 copy.68
  14.1 3.8 %collective-permute-start.1 = (bf16[68,16,4]{0,1,2:T(8,128)(2,1)S(1)}, bf16[68,16,4]{0,1,2:T(8,128)(2,1)S(1)}, u32[]{:S(2)}, u32[]{:S(2)}) collective-permute-start(bf16[68,16,4]{0,1,2:T(8,128)(2,1)S(1)} %copy.68), channel_id=1, source_target_pairs={{16,0},{32,16},{48,32},{64,48},{80,64},{96,80},{112,96},{128,112},... | collective-permute-start | bytes 26120 | tf_op jit(solution)/shard_map/ppermute | solution.py:22
  18.1 0.5 collective-permute-done
  18.6 0.3 copy.69
  19.0 0.3 copy.70
  19.3 0.6 pad_maximum_fusion.4
  19.9 3.6 %collective-permute-start.2 = (bf16[68,4,264]{2,1,0:T(4,128)(2,1)S(1)}, bf16[68,4,264]{2,1,0:T(4,128)(2,1)S(1)}, u32[]{:S(2)}, u32[]{:S(2)}) collective-permute-start(bf16[68,4,264]{2,1,0:T(4,128)(2,1)S(1)} %get-tuple-element.34), channel_id=1, source_target_pairs={{0,2},{2,4},{4,6},{6,8},{8,10},{10,12},{12,14},{1,3},{3,5},{5,7},{... | collective-permute-start | bytes 430856 | tf_op jit(solution)/shard_map/ppermute | solution.py:21
  23.5 1.5 collective-permute-start.3
  24.9 1.2 collective-permute-done.2
  26.2 4.0 %collective-permute-done.3 = bf16[68,4,264]{2,1,0:T(4,128)(2,1)S(1)} collective-permute-done((bf16[68,4,264]{2,1,0:T(4,128)(2,1)S(1)}, bf16[68,4,264]{2,1,0:T(4,128)(2,1)S(1)}, u32[]{:S(2)}, u32[]{:S(2)}) %collective-permute-start.3) | collective-permute-done | bytes 143648 | tf_op jit(solution)/shard_map/ppermute | solution.py:22
  30.7 1.3 maximum_convert_fusion
  32.0 2.6 %fusion.30 = f32[65,22,262]{2,1,0:T(8,128)S(1)} fusion(f32[68,24,264]{2,1,0:T(8,128)S(1)} %maximum_convert_fusion, f32[22,262]{1,0:T(8,128)S(1)} %get-tuple-element.59, f32[22,262]{1,0:T(8,128)S(1)} %get-tuple-element.32, f32[22,262]{1,0:T(8,128)S(1)} %get-tuple-element.58, f32[22,262]{1,0:T(8,128)S(1)} %get-tuple-element.22, ...), kind=kLoop, calls=%fused_computation.41 | loop fusion | flops 4870580 | bytes 9107120 | tf_op jit(solution)/shard_map/sub | solution.py:57
  34.7 2.6 %fusion.21 = f32[65,20,260]{2,1,0:T(8,128)S(1)} fusion(f32[65,22,262]{2,1,0:T(8,128)S(1)} %fusion.30, f32[20,260]{1,0:T(8,128)S(1)} %get-tuple-element.61, f32[20,260]{1,0:T(8,128)S(1)} %get-tuple-element.30, f32[20,260]{1,0:T(8,128)S(1)} %get-tuple-element.60, f32[20,260]{1,0:T(8,128)S(1)} %get-tuple-element.18, f32[20,260]{1,0:T(8,128)S(1)} %convert_bitcast_fusion.1), kind=kLoop, calls=%fused_computation.28 | loop fusion | flops 4394000 | bytes 8216000 | tf_op jit(solution)/shard_map/sub | solution.py:57
  37.4 2.6 %fusion.12 = f32[65,18,258]{2,1,0:T(8,128)S(1)} fusion(f32[65,20,260]{2,1,0:T(8,128)S(1)} %fusion.21, f32[18,258]{1,0:T(8,128)S(1)} %get-tuple-element.63, f32[18,258]{1,0:T(8,128)S(1)} %get-tuple-element.28, f32[18,258]{1,0:T(8,128)S(1)} %get-tuple-element.62, f32[18,258]{1,0:T(8,128)S(1)} %get-tuple-element.14, f32[18,258]{1,0:T(8,128)S(1)} %convert_bitcast_fusion), kind=kLoop, calls=%fused_computation.15 | loop fusion | flops 3924180 | bytes 7337520 | tf_op jit(solution)/shard_map/sub | solution.py:57
  40.1 1.2 fusion.56
  41.3 1.0 copy.84
  42.4 0.4 fusion.69
  43.0 0.3 fusion.118
  43.3 0.4 pad_maximum_fusion.1
  43.8 0.9 reshape.150
  44.7 14.7 %all-to-all-start = ((f32[128,1,384]{2,1,0:T(1,128)}), f32[128,1,384]{2,1,0:T(1,128)S(1)}, u32[]{:S(2)}, u32[]{:S(2)}) async-start(f32[128,1,384]{2,1,0:T(1,128)} %reshape.150), calls=%async_computation | async-start | bytes 393216 | tf_op jit(solution)/shard_map/all_to_all | solution.py:30
  59.5 1.3 concatenate.39
  60.8 1.0 concatenate.38
  61.9 1.3 pad_maximum_fusion
  63.2 8.0 %all-to-all-done = f32[128,1,384]{2,1,0:T(1,128)S(1)} async-done(((f32[128,1,384]{2,1,0:T(1,128)}), f32[128,1,384]{2,1,0:T(1,128)S(1)}, u32[]{:S(2)}, u32[]{:S(2)}) %all-to-all-start) | async-done | bytes 196640 | tf_op jit(solution)/shard_map/all_to_all | solution.py:30
  71.1 0.5 broadcast.165
  71.7 1.1 reduce.2
  73.5 0.3 fusion.65
  73.9 3.0 %fusion = f32[64,256]{1,0:T(8,128)S(1)} fusion(s32[16384]{0:T(1024)S(1)} %get-tuple-element.55, bf16[16,16384]{1,0:T(8,128)(2,1)S(1)} %get-tuple-element.49, bf16[16,16384]{1,0:T(8,128)(2,1)S(1)} %get-tuple-element.50, bf16[16,16384]{1,0:T(8,128)(2,1)S(1)} %get-tuple-element.51, bf16[16,16384]{1,0:T(8,128)(2,1)S(1)} %get-tuple-element.48), kind=kOutput, calls=%fused_computation.1 | convolution fusion | flops 549453824 | bytes 2228224 | tf_op jit(solution)/shard_map/dot_general | solution.py:161
  76.9 0.2 convolution_bitcast_fusion.3
  77.2 1.7 %fusion.66 = f32[64,128]{1,0:T(8,128)S(1)} fusion(bf16[128,4096]{1,0:T(8,128)(2,1)} %all-gather.5.cloned.1.call-done, bf16[64,4096]{1,0:T(8,128)(2,1)S(1)} %bitcast.200, f32[4096]{0:T(1024)S(1)} %bitcast.207), kind=kOutput, calls=%fused_computation.102 | convolution fusion | flops 67895296 | bytes 1622016 | tf_op jit(solution)/shard_map/dot_general | solution.py:172
  78.9 11.4 %all-reduce.2 = (f32[64]{0:T(128)S(1)}, f32[64,128]{1,0:T(8,128)S(1)}) all-reduce(f32[64]{0:T(128)S(1)} %convolution_bitcast_fusion.3, f32[64,128]{1,0:T(8,128)S(1)} %fusion.66), channel_id=1, replica_groups=mesh['lon_0'=4,'lon_1'=4,'lat'=8,'mem'=2] {'lon_0'}, use_global_device_ids=true, to_apply=%region_4.5 | all-reduce | flops 8256 | bytes 66048 | tf_op jit(solution)/shard_map/psum | solution.py:36
  90.3 11.9 %all-reduce.1 = (f32[64]{0:T(128)S(1)}, f32[64,128]{1,0:T(8,128)S(1)}) all-reduce(f32[64]{0:T(128)S(1)} %get-tuple-element.6, f32[64,128]{1,0:T(8,128)S(1)} %get-tuple-element.7), channel_id=1, replica_groups=mesh['lon_0'=4,'lon_1'=4,'lat'=8,'mem'=2] {'lon_1'}, use_global_device_ids=true, to_apply=%region_5.6 | all-reduce | flops 8256 | bytes 66048 | tf_op jit(solution)/shard_map/psum | solution.py:36
  102.4 21.2 %all-reduce = (f32[64,1]{1,0:T(8,128)S(1)}, f32[64,128]{1,0:T(8,128)S(1)}) all-reduce(f32[64,1]{1,0:T(8,128)S(1)} %copy.74, f32[64,128]{1,0:T(8,128)S(1)} %get-tuple-element.5), channel_id=1, replica_groups=mesh['lon_0'=4,'lon_1'=4,'lat'=8,'mem'=2] {'lat'}, use_global_device_ids=true, to_apply=%region_6.7 | all-reduce | flops 8256 | bytes 66048 | tf_op jit(solution)/shard_map/psum | solution.py:36
  123.6 21.1 %all_gather.11 = f32[128,129]{1,0:T(8,128)S(1)} all-gather(f32[64,129]{1,0:T(8,128)S(1)} %pad_maximum_fusion.5), channel_id=1, replica_groups=mesh['lon_0'=4,'lon_1'=4,'lat'=8,'mem'=2] {'mem'}, dimensions={0}, use_global_device_ids=true | all-gather | bytes 99072 | tf_op jit(solution)/shard_map/all_gather | solution.py:45
  144.9 0.6 reduce_max.9
  145.5 0.8 fusion.50
  146.4 0.9 fusion.96
  147.4 0.2 fusion.49
  148.0 0.2 fusion.48
  148.5 0.2 fusion.122
  148.7 0.2 fusion.47
  148.9 0.2 fusion.125
  149.9 0.2 fusion.124
  150.1 0.2 fusion.46
  150.3 0.2 fusion.127
  150.5 0.2 fusion.126
  150.8 0.2 fusion.45
  151.2 0.2 fusion.128
  151.4 0.2 fusion.44
  152.0 0.2 fusion.43
  152.2 0.3 convolution_divide_fusion
  152.9 4.2 %reshape.129 = bf16[3,128,4096]{2,1,0:T(8,128)(2,1)S(1)} reshape(bf16[3,128,16,256]{3,2,1,0:T(8,128)(2,1)} %all-gather.3.cloned.1.call-done) | data formatting | bytes 6291456 | tf_op jit(solution)/shard_map/reshape | solution.py:195
  157.1 2.3 %fusion.5 = bf16[3,64,4096]{2,1,0:T(8,128)(2,1)S(1)} fusion(bf16[3,128,4096]{2,1,0:T(8,128)(2,1)S(1)} %reshape.129, bf16[2,64,4096]{2,1,0:T(8,128)(2,1)} %concatenate.39, bf16[1,64,4096]{2,1,0:T(8,128)(2,1)} %concatenate.38, f32[4096]{0:T(1024)S(1)} %bitcast.210, f32[128,128]{0,1:T(8,128)S(1)} %convolution_divide_fusion, s32[]{:T(128)S(6)} %select_n.47), kind=kOutput, calls=%fused_computation.7 | convolution fusion | flops 206061568 | bytes 6340612 | tf_op jit(solution)/shard_map/nk,snc->skc/dot_general | solution.py:196
  159.4 1.6 copy.87
  161.0 0.5 fusion.6
  161.5 0.6 maximum_add_fusion
  (76 shorter events, 4.5 us)
Async XLA Ops:
  7.2 10.8 %copy-start.5 = (f32[128,64]{0,1:T(8,128)S(1)}, f32[128,64]{0,1:T(8,128)}, u32[]{:S(2)}) copy-start(f32[128,64]{0,1:T(8,128)} %param.20) | copy-start | bytes 98308
  7.2 10.7 %copy-start.8 = (s32[128]{0:T(128)S(1)}, s32[128]{0:T(128)}, u32[]{:S(2)}) copy-start(s32[128]{0:T(128)} %param.23) | copy-start | bytes 1540
  7.2 10.8 %copy-start.9 = (s32[128,1]{0,1:T(1,128)S(1)}, s32[128,1]{0,1:T(1,128)}, u32[]{:S(2)}) copy-start(s32[128,1]{0,1:T(1,128)} %param.22) | copy-start | bytes 1540
  7.2 10.9 %copy-start.6 = (s32[128,64]{0,1:T(8,128)S(1)}, s32[128,64]{0,1:T(8,128)}, u32[]{:S(2)}) copy-start(s32[128,64]{0,1:T(8,128)} %param.21) | copy-start | bytes 98308
  7.2 70.0 %all-gather.5.cloned.1.call-start = ((), (), s32[]{:S(2)}) async-start(), calls=%async_computation.2 | async-start | bytes 1572864 | tf_op jit(solution)/shard_map/all_gather | solution.py:171
  11.7 6.9 %collective-permute-start = (bf16[68,16,4]{0,1,2:T(8,128)(2,1)S(1)}, bf16[68,16,4]{0,1,2:T(8,128)(2,1)S(1)}, u32[]{:S(2)}, u32[]{:S(2)}) collective-permute-start(bf16[68,16,4]{0,1,2:T(8,128)(2,1)S(1)} %copy.67), channel_id=1, source_target_pairs={{0,16},{16,32},{32,48},{48,64},{64,80},{80,96},{96,112},{112,128},... | collective-permute-start | bytes 26120 | tf_op jit(solution)/shard_map/ppermute | solution.py:21
  14.1 4.8 %collective-permute-start.1 = (bf16[68,16,4]{0,1,2:T(8,128)(2,1)S(1)}, bf16[68,16,4]{0,1,2:T(8,128)(2,1)S(1)}, u32[]{:S(2)}, u32[]{:S(2)}) collective-permute-start(bf16[68,16,4]{0,1,2:T(8,128)(2,1)S(1)} %copy.68), channel_id=1, source_target_pairs={{16,0},{32,16},{48,32},{64,48},{80,64},{96,80},{112,96},{128,112},... | collective-permute-start | bytes 26120 | tf_op jit(solution)/shard_map/ppermute | solution.py:22
  19.9 6.3 %collective-permute-start.2 = (bf16[68,4,264]{2,1,0:T(4,128)(2,1)S(1)}, bf16[68,4,264]{2,1,0:T(4,128)(2,1)S(1)}, u32[]{:S(2)}, u32[]{:S(2)}) collective-permute-start(bf16[68,4,264]{2,1,0:T(4,128)(2,1)S(1)} %get-tuple-element.34), channel_id=1, source_target_pairs={{0,2},{2,4},{4,6},{6,8},{8,10},{10,12},{12,14},{1,3},{3,5},{5,7},{... | collective-permute-start | bytes 430856 | tf_op jit(solution)/shard_map/ppermute | solution.py:21
  23.5 6.7 %collective-permute-start.3 = (bf16[68,4,264]{2,1,0:T(4,128)(2,1)S(1)}, bf16[68,4,264]{2,1,0:T(4,128)(2,1)S(1)}, u32[]{:S(2)}, u32[]{:S(2)}) collective-permute-start(bf16[68,4,264]{2,1,0:T(4,128)(2,1)S(1)} %get-tuple-element.35), channel_id=1, source_target_pairs={{2,0},{4,2},{6,4},{8,6},{10,8},{12,10},{14,12},{3,1},{5,3},{7,5},{... | collective-permute-start | bytes 430856 | tf_op jit(solution)/shard_map/ppermute | solution.py:22
  41.2 35.6 %copy-start.1 = (f32[65,16,256]{2,1,0:T(8,128)}, f32[65,16,256]{2,1,0:T(8,128)S(1)}, u32[]{:S(2)}) copy-start(f32[65,16,256]{2,1,0:T(8,128)S(1)} %fusion.56) | copy-start | bytes 3194884
  41.3 1.2 copy-start.7
  42.4 17.0 %copy-start.3 = (s32[16,256]{1,0:T(8,128)S(1)}, s32[16,256]{1,0:T(8,128)}, u32[]{:S(2)}) copy-start(s32[16,256]{1,0:T(8,128)} %param.18) | copy-start | bytes 49156
  42.4 17.1 %copy-start.2 = (bf16[2,64,16,256]{3,2,1,0:T(8,128)(2,1)S(1)}, bf16[2,64,16,256]{3,2,1,0:T(8,128)(2,1)}, u32[]{:S(2)}) copy-start(bf16[2,64,16,256]{3,2,1,0:T(8,128)(2,1)} %param.14) | copy-start | bytes 3145732
  44.7 26.5 %all-to-all-start = ((f32[128,1,384]{2,1,0:T(1,128)}), f32[128,1,384]{2,1,0:T(1,128)S(1)}, u32[]{:S(2)}, u32[]{:S(2)}) async-start(f32[128,1,384]{2,1,0:T(1,128)} %reshape.150), calls=%async_computation | async-start | bytes 393216 | tf_op jit(solution)/shard_map/all_to_all | solution.py:30
  59.4 93.5 %all-gather.3.cloned.1.call-start = ((), (), s32[]{:S(2)}) async-start(), calls=%async_computation.1 | async-start | bytes 4718592 | tf_op jit(solution)/shard_map/all_gather | solution.py:193
  73.9 3.1 %copy-start = (bf16[8,8,16,256]{3,1,2,0:T(8,128)(2,1)S(1)}, bf16[8,8,16,256]{3,1,2,0:T(8,128)(2,1)}, u32[]{:S(2)}) copy-start(bf16[8,8,16,256]{3,1,2,0:T(8,128)(2,1)} %copy.84) | copy-start | bytes 1572868
  159.4 2.1 %slice-start = ((f32[65,16,256]{2,1,0:T(8,128)}), f32[1,16,256]{2,1,0:T(8,128)S(1)}, s32[]{:S(2)}) async-start(f32[65,16,256]{2,1,0:T(8,128)} %copy-done.1), calls=%async_computation.3 | async-start | bytes 32768 | tf_op jit(solution)/shard_map/slice | solution.py:124
  159.4 2.1 %copy-start.4 = (f32[2,16,256]{2,1,0:T(8,128)S(1)}, f32[2,16,256]{2,1,0:T(8,128)}, u32[]{:S(2)}) copy-start(f32[2,16,256]{2,1,0:T(8,128)} %param.15) | copy-start | bytes 98308
Sparse Core Ops, SparseCore 0:
  42.5 19.9 all-gather.4
  64.9 20.6 all-gather.2
where the time goes:
time: 170 us; the launch traced here: 169 us
  blocking collectives  65.6 us (39%)
  starting transfers between devices  25.7 us (15%)
  other arithmetic  18.3 us (11%)
  local copies, waits for them, and re-layouts  15.7 us (9%)
  between operations  15.4 us (9%)
  matrix products  14.5 us (9%)
  waiting for transfers between devices  13.7 us (8%)
    psum x3, blocking collectives, over_axes(): x = lax.psum(x, axis)  44.5 us
    all_gather x1, blocking collectives, side_by_side(): out = lax.all_gather(both, axis, axis=dim, tiled=True)  21.1 us
    all_to_all x1, starting transfers between devices, sent_together(): lax.all_to_all(both, axis, split_axis=split_dim, concat_axis=concat_dim,...  14.7 us
    sub x4, other arithmetic, upwind(): return center - wet_mask * tendency  8.92 us
    all_to_all x1, waiting for transfers between devices, sent_together(): lax.all_to_all(both, axis, split_axis=split_dim, concat_axis=concat_dim,...  7.95 us
    unnamed x30, local copies, waits for them, and re-layouts  5.93 us
    ppermute x2, starting transfers between devices, with_halo(): before = lax.ppermute(last, axis, up)  5.65 us
    ppermute x2, starting transfers between devices, with_halo(): after = lax.ppermute(leading, axis, down)  5.26 us
  transfers between devices with their start and end apart: 7, of which 4 were waited for; matrix products, arithmetic and copies ran while one was open for 13% of the time, Pallas kernels for 0%

commit v1 on v0

--- a/solution.py
+++ b/solution.py
@@ -33,7 +33,7 @@
 
 def over_axes(x, axes):
     for axis in axes:
-        x = lax.psum(x, axis)
+        x = jnp.sum(lax.all_gather(x, axis), axis=0)
     return x
 
 

time: 170 us -> 193 us (1.14)
  blocking collectives: 65.6 us -> 88 us
  waiting for transfers between devices: 13.7 us -> 10 us
  local copies, waits for them, and re-layouts: 15.7 us -> 18.4 us
  between operations: 15.4 us -> 17.4 us
    psum x3 -> x0, blocking collectives: 44.5 us -> none  [over_axes(): x = lax.psum(x, axis)]
    all_gather x0 -> x3, blocking collectives: none -> 37.3 us  [over_axes(): x = jnp.sum(lax.all_gather(x, axis), axis=0)]
    unnamed x0 -> x3, blocking collectives: none -> 25.9 us
    all_gather x1, blocking collectives: 21.1 us -> 24.8 us  [side_by_side(): out = lax.all_gather(both, axis, axis=dim, tiled=True)]
    all_to_all x1, waiting for transfers between devices: 7.95 us -> 4.25 us  [sent_together(): lax.all_to_all(both, axis, split_axis=split_dim, concat_axis=concat_dim,...]
    unnamed x30 -> x46, local copies, waits for them, and re-layouts: 5.93 us -> 8.48 us
where the time goes in v1:
time: 193 us
  blocking collectives  88 us (46%)
  starting transfers between devices  25.7 us (13%)
  local copies, waits for them, and re-layouts  18.4 us (10%)
  other arithmetic  18.4 us (10%)
  between operations  17.4 us (9%)
  matrix products  14.5 us (8%)
  waiting for transfers between devices  10 us (5%)
    all_gather x3, blocking collectives, over_axes(): x = jnp.sum(lax.all_gather(x, axis), axis=0)  37.3 us
    unnamed x3, blocking collectives  25.9 us
    all_gather x1, blocking collectives, side_by_side(): out = lax.all_gather(both, axis, axis=dim, tiled=True)  24.8 us
    all_to_all x1, starting transfers between devices, sent_together(): lax.all_to_all(both, axis, split_axis=split_dim, concat_axis=concat_dim,...  14.7 us
    sub x4, other arithmetic, upwind(): return center - wet_mask * tendency  8.92 us
    unnamed x46, local copies, waits for them, and re-layouts  8.48 us
    ppermute x2, starting transfers between devices, with_halo(): before = lax.ppermute(last, axis, up)  5.65 us
    ppermute x2, starting transfers between devices, with_halo(): after = lax.ppermute(leading, axis, down)  5.26 us
  transfers between devices with their start and end apart: 7, of which 4 were waited for; matrix products, arithmetic and copies ran while one was open for 13% of the time, Pallas kernels for 0%

profile of v1, /device:TPU:1, one launch (start us, length us, event | category | flops | bytes accessed | tf_op | source)
XLA Modules:
  0.0 192.5 jit_solution(17746795382664871909)
XLA Ops:
  7.3 1.1 convert_dynamic-update-slice_fusion
  8.3 0.7 bitcast_dynamic-update-slice_fusion.3
  9.1 0.7 bitcast_dynamic-update-slice_fusion.2
  9.8 0.7 bitcast_dynamic-update-slice_fusion.1
  10.5 0.7 bitcast_dynamic-update-slice_fusion
  11.4 0.3 copy.68
  11.7 2.1 %collective-permute-start = (bf16[68,16,4]{0,1,2:T(8,128)(2,1)S(1)}, bf16[68,16,4]{0,1,2:T(8,128)(2,1)S(1)}, u32[]{:S(2)}, u32[]{:S(2)}) collective-permute-start(bf16[68,16,4]{0,1,2:T(8,128)(2,1)S(1)} %copy.68), channel_id=1, source_target_pairs={{0,16},{16,32},{32,48},{48,64},{64,80},{80,96},{96,112},{112,128},... | collective-permute-start | bytes 26120 | tf_op jit(solution)/shard_map/ppermute | solution.py:21
  13.8 0.3 copy.69
  14.1 3.8 %collective-permute-start.1 = (bf16[68,16,4]{0,1,2:T(8,128)(2,1)S(1)}, bf16[68,16,4]{0,1,2:T(8,128)(2,1)S(1)}, u32[]{:S(2)}, u32[]{:S(2)}) collective-permute-start(bf16[68,16,4]{0,1,2:T(8,128)(2,1)S(1)} %copy.69), channel_id=1, source_target_pairs={{16,0},{32,16},{48,32},{64,48},{80,64},{96,80},{112,96},{128,112},... | collective-permute-start | bytes 26120 | tf_op jit(solution)/shard_map/ppermute | solution.py:22
  18.1 0.5 collective-permute-done
  18.6 0.3 copy.70
  19.0 0.3 copy.71
  19.3 0.6 pad_maximum_fusion.4
  19.9 3.6 %collective-permute-start.2 = (bf16[68,4,264]{2,1,0:T(4,128)(2,1)S(1)}, bf16[68,4,264]{2,1,0:T(4,128)(2,1)S(1)}, u32[]{:S(2)}, u32[]{:S(2)}) collective-permute-start(bf16[68,4,264]{2,1,0:T(4,128)(2,1)S(1)} %get-tuple-element.28), channel_id=1, source_target_pairs={{0,2},{2,4},{4,6},{6,8},{8,10},{10,12},{12,14},{1,3},{3,5},{5,7},{... | collective-permute-start | bytes 430856 | tf_op jit(solution)/shard_map/ppermute | solution.py:21
  23.5 1.5 collective-permute-start.3
  24.9 1.2 collective-permute-done.2
  26.2 4.0 %collective-permute-done.3 = bf16[68,4,264]{2,1,0:T(4,128)(2,1)S(1)} collective-permute-done((bf16[68,4,264]{2,1,0:T(4,128)(2,1)S(1)}, bf16[68,4,264]{2,1,0:T(4,128)(2,1)S(1)}, u32[]{:S(2)}, u32[]{:S(2)}) %collective-permute-start.3) | collective-permute-done | bytes 143648 | tf_op jit(solution)/shard_map/ppermute | solution.py:22
  30.7 1.3 maximum_convert_fusion
  32.0 2.6 %fusion.30 = f32[65,22,262]{2,1,0:T(8,128)S(1)} fusion(f32[68,24,264]{2,1,0:T(8,128)S(1)} %maximum_convert_fusion, f32[22,262]{1,0:T(8,128)S(1)} %get-tuple-element.53, f32[22,262]{1,0:T(8,128)S(1)} %get-tuple-element.26, f32[22,262]{1,0:T(8,128)S(1)} %get-tuple-element.52, f32[22,262]{1,0:T(8,128)S(1)} %get-tuple-element.16, ...), kind=kLoop, calls=%fused_computation.41 | loop fusion | flops 4870580 | bytes 9107120 | tf_op jit(solution)/shard_map/sub | solution.py:57
  34.7 2.6 %fusion.21 = f32[65,20,260]{2,1,0:T(8,128)S(1)} fusion(f32[65,22,262]{2,1,0:T(8,128)S(1)} %fusion.30, f32[20,260]{1,0:T(8,128)S(1)} %get-tuple-element.55, f32[20,260]{1,0:T(8,128)S(1)} %get-tuple-element.24, f32[20,260]{1,0:T(8,128)S(1)} %get-tuple-element.54, f32[20,260]{1,0:T(8,128)S(1)} %get-tuple-element.12, f32[20,260]{1,0:T(8,128)S(1)} %convert_bitcast_fusion.1), kind=kLoop, calls=%fused_computation.28 | loop fusion | flops 4394000 | bytes 8216000 | tf_op jit(solution)/shard_map/sub | solution.py:57
  37.4 2.6 %fusion.12 = f32[65,18,258]{2,1,0:T(8,128)S(1)} fusion(f32[65,20,260]{2,1,0:T(8,128)S(1)} %fusion.21, f32[18,258]{1,0:T(8,128)S(1)} %get-tuple-element.57, f32[18,258]{1,0:T(8,128)S(1)} %get-tuple-element.22, f32[18,258]{1,0:T(8,128)S(1)} %get-tuple-element.56, f32[18,258]{1,0:T(8,128)S(1)} %get-tuple-element.8, f32[18,258]{1,0:T(8,128)S(1)} %convert_bitcast_fusion), kind=kLoop, calls=%fused_computation.15 | loop fusion | flops 3924180 | bytes 7337520 | tf_op jit(solution)/shard_map/sub | solution.py:57
  40.1 1.2 fusion.56
  41.3 1.1 copy.87
  42.5 0.4 fusion.69
  43.1 0.3 fusion.118
  43.3 0.4 pad_maximum_fusion.1
  43.8 0.9 reshape.171
  44.7 14.7 %all-to-all-start = ((f32[128,1,384]{2,1,0:T(1,128)}), f32[128,1,384]{2,1,0:T(1,128)S(1)}, u32[]{:S(2)}, u32[]{:S(2)}) async-start(f32[128,1,384]{2,1,0:T(1,128)} %reshape.171), calls=%async_computation | async-start | bytes 393216 | tf_op jit(solution)/shard_map/all_to_all | solution.py:30
  59.5 0.6 dynamic-slice
  60.1 0.6 dynamic-slice.1
  61.9 0.6 dynamic-slice.2
  63.2 1.3 concatenate.39
  64.5 1.1 concatenate.38
  65.7 1.3 pad_maximum_fusion
  67.0 4.3 %all-to-all-done = f32[128,1,384]{2,1,0:T(1,128)S(1)} async-done(((f32[128,1,384]{2,1,0:T(1,128)}), f32[128,1,384]{2,1,0:T(1,128)S(1)}, u32[]{:S(2)}, u32[]{:S(2)}) %all-to-all-start) | async-done | bytes 196640 | tf_op jit(solution)/shard_map/all_to_all | solution.py:30
  71.2 0.5 broadcast.168
  71.7 1.1 reduce.2
  73.6 0.3 fusion.65
  74.0 3.0 %fusion = f32[64,256]{1,0:T(8,128)S(1)} fusion(s32[16384]{0:T(1024)S(1)} %get-tuple-element.49, bf16[16,16384]{1,0:T(8,128)(2,1)S(1)} %get-tuple-element.43, bf16[16,16384]{1,0:T(8,128)(2,1)S(1)} %get-tuple-element.44, bf16[16,16384]{1,0:T(8,128)(2,1)S(1)} %get-tuple-element.45, bf16[16,16384]{1,0:T(8,128)(2,1)S(1)} %get-tuple-element.42), kind=kOutput, calls=%fused_computation.1 | convolution fusion | flops 549453824 | bytes 2228224 | tf_op jit(solution)/shard_map/dot_general | solution.py:161
  77.0 0.2 convolution_bitcast_fusion.3
  77.5 6.3 %all-reduce = f32[256]{0:T(256)S(1)} all-reduce(f32[256]{0:T(256)S(1)} %dynamic-update-slice), channel_id=5, replica_groups=mesh['lon_0'=4,'lon_1'=4,'lat'=8,'mem'=2] {'lon_0'}, use_global_device_ids=true, to_apply=%add | all-reduce | flops 256 | bytes 2048
  83.8 0.2 dynamic-update-slice.1
  84.1 6.8 %all-reduce.1 = f32[256]{0:T(256)S(1)} all-reduce(f32[256]{0:T(256)S(1)} %dynamic-update-slice.1), channel_id=6, replica_groups=mesh['lon_0'=4,'lon_1'=4,'lat'=8,'mem'=2] {'lon_1'}, use_global_device_ids=true, to_apply=%add.1 | all-reduce | flops 256 | bytes 2048
  90.9 0.2 dynamic-update-slice.2
  91.2 12.9 %all-reduce.2 = f32[512]{0:T(512)S(1)} all-reduce(f32[512]{0:T(512)S(1)} %dynamic-update-slice.2), channel_id=7, replica_groups=mesh['lon_0'=4,'lon_1'=4,'lat'=8,'mem'=2] {'lat'}, use_global_device_ids=true, to_apply=%add.2 | all-reduce | flops 512 | bytes 4096
  104.3 1.7 fusion.66
  106.0 9.1 %all-gather = f32[256,128]{1,0:T(8,128)S(1)} all-gather(f32[64,128]{1,0:T(8,128)S(1)} %fusion.66), channel_id=2, replica_groups=mesh['lon_0'=4,'lon_1'=4,'lat'=8,'mem'=2] {'lon_0'}, dimensions={0}, use_global_device_ids=true | all-gather | bytes 163840 | tf_op jit(solution)/shard_map/all_gather | solution.py:36
  115.2 9.1 %all-gather.1 = f32[256,128]{1,0:T(8,128)S(1)} all-gather(f32[64,128]{1,0:T(8,128)S(1)} %reduce_sum.76), channel_id=3, replica_groups=mesh['lon_0'=4,'lon_1'=4,'lat'=8,'mem'=2] {'lon_1'}, dimensions={0}, use_global_device_ids=true | all-gather | bytes 163840 | tf_op jit(solution)/shard_map/all_gather | solution.py:36
  124.3 19.0 %all-gather.2 = f32[512,128]{1,0:T(8,128)S(1)} all-gather(f32[64,128]{1,0:T(8,128)S(1)} %reduce_sum.77), channel_id=4, replica_groups=mesh['lon_0'=4,'lon_1'=4,'lat'=8,'mem'=2] {'lat'}, dimensions={0}, use_global_device_ids=true | all-gather | bytes 294912 | tf_op jit(solution)/shard_map/all_gather | solution.py:36
  143.3 24.8 %all_gather.59 = f32[128,129]{1,0:T(8,128)S(1)} all-gather(f32[64,129]{1,0:T(8,128)S(1)} %pad_maximum_fusion.5), channel_id=1, replica_groups=mesh['lon_0'=4,'lon_1'=4,'lat'=8,'mem'=2] {'mem'}, dimensions={0}, use_global_device_ids=true | all-gather | bytes 99072 | tf_op jit(solution)/shard_map/all_gather | solution.py:45
  168.4 0.6 reduce_max.9
  169.0 0.8 fusion.50
  169.8 0.9 fusion.96
  170.9 0.2 fusion.49
  171.5 0.2 fusion.48
  172.2 0.2 fusion.47
  173.6 0.2 fusion.46
  175.5 0.2 fusion.43
  175.7 0.3 convolution_divide_fusion
  176.4 4.2 %reshape.129 = bf16[3,128,4096]{2,1,0:T(8,128)(2,1)S(1)} reshape(bf16[3,128,16,256]{3,2,1,0:T(8,128)(2,1)} %all-gather.9.cloned.1.call-done) | data formatting | bytes 6291456 | tf_op jit(solution)/shard_map/reshape | solution.py:195
  180.6 2.3 %fusion.5 = bf16[3,64,4096]{2,1,0:T(8,128)(2,1)S(1)} fusion(bf16[3,128,4096]{2,1,0:T(8,128)(2,1)S(1)} %reshape.129, bf16[2,64,4096]{2,1,0:T(8,128)(2,1)} %concatenate.39, bf16[1,64,4096]{2,1,0:T(8,128)(2,1)} %concatenate.38, f32[4096]{0:T(1024)S(1)} %bitcast.219, f32[128,128]{0,1:T(8,128)S(1)} %convolution_divide_fusion, s32[]{:T(128)S(6)} %select_n.47), kind=kOutput, calls=%fused_computation.7 | convolution fusion | flops 206061568 | bytes 6340612 | tf_op jit(solution)/shard_map/nk,snc->skc/dot_general | solution.py:196
  182.9 1.6 copy.90
  184.5 0.5 fusion.6
  185.0 0.6 maximum_add_fusion
  (103 shorter events, 6.7 us)
Async XLA Ops:
  7.2 10.8 %copy-start.5 = (f32[128,64]{0,1:T(8,128)S(1)}, f32[128,64]{0,1:T(8,128)}, u32[]{:S(2)}) copy-start(f32[128,64]{0,1:T(8,128)} %param.20) | copy-start | bytes 98308
  7.2 10.7 %copy-start.8 = (s32[128]{0:T(128)S(1)}, s32[128]{0:T(128)}, u32[]{:S(2)}) copy-start(s32[128]{0:T(128)} %param.23) | copy-start | bytes 1540
  7.2 10.8 %copy-start.9 = (s32[128,1]{0,1:T(1,128)S(1)}, s32[128,1]{0,1:T(1,128)}, u32[]{:S(2)}) copy-start(s32[128,1]{0,1:T(1,128)} %param.22) | copy-start | bytes 1540
  7.2 10.9 %copy-start.6 = (s32[128,64]{0,1:T(8,128)S(1)}, s32[128,64]{0,1:T(8,128)}, u32[]{:S(2)}) copy-start(s32[128,64]{0,1:T(8,128)} %param.21) | copy-start | bytes 98308
  7.2 97.1 %all-gather.11.cloned.1.call-start = ((), (), s32[]{:S(2)}) async-start(), calls=%async_computation.2 | async-start | bytes 1572864 | tf_op jit(solution)/shard_map/all_gather | solution.py:171
  11.7 6.9 %collective-permute-start = (bf16[68,16,4]{0,1,2:T(8,128)(2,1)S(1)}, bf16[68,16,4]{0,1,2:T(8,128)(2,1)S(1)}, u32[]{:S(2)}, u32[]{:S(2)}) collective-permute-start(bf16[68,16,4]{0,1,2:T(8,128)(2,1)S(1)} %copy.68), channel_id=1, source_target_pairs={{0,16},{16,32},{32,48},{48,64},{64,80},{80,96},{96,112},{112,128},... | collective-permute-start | bytes 26120 | tf_op jit(solution)/shard_map/ppermute | solution.py:21
  14.1 4.8 %collective-permute-start.1 = (bf16[68,16,4]{0,1,2:T(8,128)(2,1)S(1)}, bf16[68,16,4]{0,1,2:T(8,128)(2,1)S(1)}, u32[]{:S(2)}, u32[]{:S(2)}) collective-permute-start(bf16[68,16,4]{0,1,2:T(8,128)(2,1)S(1)} %copy.69), channel_id=1, source_target_pairs={{16,0},{32,16},{48,32},{64,48},{80,64},{96,80},{112,96},{128,112},... | collective-permute-start | bytes 26120 | tf_op jit(solution)/shard_map/ppermute | solution.py:22
  19.9 6.3 %collective-permute-start.2 = (bf16[68,4,264]{2,1,0:T(4,128)(2,1)S(1)}, bf16[68,4,264]{2,1,0:T(4,128)(2,1)S(1)}, u32[]{:S(2)}, u32[]{:S(2)}) collective-permute-start(bf16[68,4,264]{2,1,0:T(4,128)(2,1)S(1)} %get-tuple-element.28), channel_id=1, source_target_pairs={{0,2},{2,4},{4,6},{6,8},{8,10},{10,12},{12,14},{1,3},{3,5},{5,7},{... | collective-permute-start | bytes 430856 | tf_op jit(solution)/shard_map/ppermute | solution.py:21
  23.5 6.7 %collective-permute-start.3 = (bf16[68,4,264]{2,1,0:T(4,128)(2,1)S(1)}, bf16[68,4,264]{2,1,0:T(4,128)(2,1)S(1)}, u32[]{:S(2)}, u32[]{:S(2)}) collective-permute-start(bf16[68,4,264]{2,1,0:T(4,128)(2,1)S(1)} %get-tuple-element.29), channel_id=1, source_target_pairs={{2,0},{4,2},{6,4},{8,6},{10,8},{12,10},{14,12},{3,1},{5,3},{7,5},{... | collective-permute-start | bytes 430856 | tf_op jit(solution)/shard_map/ppermute | solution.py:22
  41.2 35.7 %copy-start.1 = (f32[65,16,256]{2,1,0:T(8,128)}, f32[65,16,256]{2,1,0:T(8,128)S(1)}, u32[]{:S(2)}) copy-start(f32[65,16,256]{2,1,0:T(8,128)S(1)} %fusion.56) | copy-start | bytes 3194884
  41.3 1.2 copy-start.7
  42.4 17.0 %copy-start.12 = (u32[256]{0:T(256)S(1)}, u32[256]{0:T(256)}, u32[]{:S(2)}) copy-start(u32[256]{0:T(256)} %constant.63) | copy-start | bytes 3076
  42.4 17.6 %copy-start.11 = (u32[256]{0:T(256)S(1)}, u32[256]{0:T(256)}, u32[]{:S(2)}) copy-start(u32[256]{0:T(256)} %constant.68) | copy-start | bytes 3076
  42.4 19.5 %copy-start.10 = (u32[256]{0:T(256)S(1)}, u32[256]{0:T(256)}, u32[]{:S(2)}) copy-start(u32[256]{0:T(256)} %constant.73) | copy-start | bytes 3076
  42.4 20.8 %copy-start.3 = (s32[16,256]{1,0:T(8,128)S(1)}, s32[16,256]{1,0:T(8,128)}, u32[]{:S(2)}) copy-start(s32[16,256]{1,0:T(8,128)} %param.18) | copy-start | bytes 49156
  42.4 20.8 %copy-start.2 = (bf16[2,64,16,256]{3,2,1,0:T(8,128)(2,1)S(1)}, bf16[2,64,16,256]{3,2,1,0:T(8,128)(2,1)}, u32[]{:S(2)}) copy-start(bf16[2,64,16,256]{3,2,1,0:T(8,128)(2,1)} %param.14) | copy-start | bytes 3145732
  44.7 26.5 %all-to-all-start = ((f32[128,1,384]{2,1,0:T(1,128)}), f32[128,1,384]{2,1,0:T(1,128)S(1)}, u32[]{:S(2)}, u32[]{:S(2)}) async-start(f32[128,1,384]{2,1,0:T(1,128)} %reshape.171), calls=%async_computation | async-start | bytes 393216 | tf_op jit(solution)/shard_map/all_to_all | solution.py:30
  59.4 117.0 %all-gather.9.cloned.1.call-start = ((), (), s32[]{:S(2)}) async-start(), calls=%async_computation.1 | async-start | bytes 4718592 | tf_op jit(solution)/shard_map/all_gather | solution.py:193
  74.0 3.1 %copy-start = (bf16[8,8,16,256]{3,1,2,0:T(8,128)(2,1)S(1)}, bf16[8,8,16,256]{3,1,2,0:T(8,128)(2,1)}, u32[]{:S(2)}) copy-start(bf16[8,8,16,256]{3,1,2,0:T(8,128)(2,1)} %copy.87) | copy-start | bytes 1572868
  182.9 2.1 %slice-start = ((f32[65,16,256]{2,1,0:T(8,128)}), f32[1,16,256]{2,1,0:T(8,128)S(1)}, s32[]{:S(2)}) async-start(f32[65,16,256]{2,1,0:T(8,128)} %copy-done.1), calls=%async_computation.3 | async-start | bytes 32768 | tf_op jit(solution)/shard_map/slice | solution.py:124
  182.9 2.1 %copy-start.4 = (f32[2,16,256]{2,1,0:T(8,128)S(1)}, f32[2,16,256]{2,1,0:T(8,128)}, u32[]{:S(2)}) copy-start(f32[2,16,256]{2,1,0:T(8,128)} %param.15) | copy-start | bytes 98308
Sparse Core Ops, SparseCore 0:
  42.6 19.9 all-gather.10
  67.1 22.2 all-gather.8
